TPU v7x, 32 devices: a whole 2x2x4 slice. The times are simulated.
32 devices in a mesh: lat: 16 (over z, x, core), chan: 2 (over y).
Axes of the slice: x: 2, y: 2, z: 4, core: 2. Of those that a mesh axis runs over, the one named last changes fastest.
Arguments:
- ocean_state: bfloat16 [384, 256, 1440], P('lat', 'chan'), may hold values from -6 to 6
- land_mask: int32 [384, 1440], P('lat', 'chan'), may hold values 0 or 1
- order_table: int32 [384], replicated, may hold values from 0 to 383, each once
- spectral_weight: bfloat16 [384, 2, 256, 256], P('lat', None, 'chan'), may hold values from -0.25 to 0.25
- inner_weight: bfloat16 [256, 512], P(None, 'chan'), may hold values from -0.375 to 0.375
- outer_weight: bfloat16 [512, 256], P('chan'), may hold values from -0.25 to 0.25
Outputs:
- layer_output: bfloat16 [384, 1440, 256], P('lat', 'chan')
Inputs may be any that keep to these rules, and one draw needn't show every extreme that they name: `order_table`: a permutation: every order from 0 to 383 stands in exactly one slot.
All inputs are finite; a program needn't handle non-finite values. Where the computation divides by a largest or mean magnitude, that divisor is 1e-20 or more. No bound on the sum of `land_mask` on one device may be relied on, other than what follows from the above.
Results may differ from a plain program's by a relative error of at most 0.0095.
Values may be sent and summed in bfloat16 or wider, within the bound.
No kernel may reach another device: no remote copies, remote signals or barrier semaphores. Data moves between devices by JAX's collectives and lax.ppermute only.
A program may use at most 128 MiB of HBM per device.

v0:
```python
import math
import jax
import jax.numpy as jnp
from jax import lax
from jax.sharding import PartitionSpec as P

NLAT = 384
NLON = 1440
MODES = 384


def fejer_weights():
    colatitude = (jnp.arange(NLAT, dtype=jnp.float32) + 0.5) * (math.pi / NLAT)
    harmonic = jnp.arange(1, NLAT // 2 + 1).astype(jnp.float32)
    series = (
        jnp.cos(2.0 * colatitude[:, None] * harmonic[None, :])
        / (4.0 * harmonic * harmonic - 1.0)[None, :]
    )
    return 2.0 / NLAT * (1.0 - 2.0 * jnp.sum(series, axis=1))


def compose(earlier, latter):
    first_mat, first_log = earlier
    second_mat, second_log = latter
    product = jnp.stack(
        [
            second_mat[0] * first_mat[0] + second_mat[1] * first_mat[2],
            second_mat[0] * first_mat[1] + second_mat[1] * first_mat[3],
            second_mat[2] * first_mat[0] + second_mat[3] * first_mat[2],
            second_mat[2] * first_mat[1] + second_mat[3] * first_mat[3],
        ]
    )
    largest = jnp.max(jnp.abs(product), axis=0, keepdims=True)
    return (product / largest, first_log + second_log + jnp.log(largest))


def legendre_rows(order_value):
    half_rows = NLAT // 2
    colatitude = (jnp.arange(half_rows, dtype=jnp.float32) + 0.5) * (math.pi / NLAT)
    cosine = jnp.cos(colatitude)
    sine_part = jnp.sin(colatitude)
    offsets = jnp.arange(MODES).astype(jnp.float32)
    order_float = order_value.astype(jnp.float32)
    degree = order_float + offsets
    beyond_start = offsets >= 1.0
    denominator = jnp.where(beyond_start, degree * degree - order_float * order_float, 1.0)
    upper_coef = jnp.sqrt((4.0 * degree * degree - 1.0) / denominator)
    previous = degree - 1.0
    lower_coef = jnp.sqrt(
        jnp.maximum(previous * previous - order_float * order_float, 0.0)
        / jnp.maximum(4.0 * previous * previous - 1.0, 1.0)
    )
    filled = jnp.ones((MODES, half_rows), jnp.float32)
    beyond_column = beyond_start[:, None]
    matrix = jnp.stack(
        [
            jnp.where(beyond_column, upper_coef[:, None] * cosine[None, :], filled),
            jnp.where(beyond_column, -(upper_coef * lower_coef)[:, None] * filled, 0.0 * filled),
            jnp.where(beyond_column, filled, 0.0 * filled),
            jnp.where(beyond_column, 0.0 * filled, filled),
        ]
    )
    log_scale = jnp.zeros((1, MODES, half_rows), jnp.float32)
    matrix, log_scale = lax.associative_scan(compose, (matrix, log_scale), axis=1)
    steps_log = 0.5 * jnp.log((2.0 * offsets + 3.0) / (2.0 * offsets + 2.0))
    cumulative = jnp.cumsum(steps_log) - steps_log
    picked = jnp.sum(jnp.where(jnp.arange(MODES) == order_value, cumulative, 0.0 * cumulative))
    start_log = 0.5 * math.log(0.5) + picked + order_float * jnp.log(sine_part)
    northern = jnp.exp(start_log[None, :] + log_scale[0]) * matrix[0]
    northern = jnp.where((offsets < MODES - order_float)[:, None], northern, 0.0 * filled)
    parity = jnp.where(jnp.arange(MODES) % 2 == 0, 1.0, -1.0).astype(jnp.float32)
    return jnp.concatenate([northern, northern[:, ::-1] * parity[:, None]], axis=1)


def fourier_tables(orders):
    longitude = jnp.arange(NLON)
    phase_index = orders[:, None] * longitude[None, :] % NLON
    angles = phase_index.astype(jnp.float32) * (2.0 * math.pi / NLON)
    cosine = jnp.cos(angles)
    sine_part = jnp.sin(angles)
    forward = (
        jnp.concatenate([cosine, -sine_part], axis=0) * (math.sqrt(2.0 * math.pi) / NLON)
    ).astype(jnp.bfloat16)
    factor = jnp.where(orders == 0, 1.0, 2.0).astype(jnp.float32) / math.sqrt(2.0 * math.pi)
    inverse = jnp.concatenate(
        [cosine * factor[:, None], -sine_part * factor[:, None]], axis=0
    ).astype(jnp.bfloat16)
    return (forward, inverse)


def mixing_blocks(weights):
    real_part = weights[:, 0]
    imag_part = weights[:, 1]
    return jnp.stack(
        [jnp.stack([real_part, imag_part], axis=1), jnp.stack([-imag_part, real_part], axis=1)],
        axis=1,
    )


def local(ocean_state, land_mask, order_table, spectral_weight, inner_weight, outer_weight):
    local_rows = ocean_state.shape[0]
    local_channels = ocean_state.shape[1]
    slots_here = spectral_weight.shape[0]
    forward, inverse = fourier_tables(order_table)
    flat_state = ocean_state.reshape(local_rows * local_channels, NLON)
    coeffs = lax.dot_general(
        flat_state, forward, (((1,), (1,)), ((), ())), preferred_element_type=jnp.float32
    )
    coeffs = coeffs.astype(jnp.bfloat16).reshape(local_rows, local_channels, 2, MODES)
    owned_coeffs = lax.all_to_all(coeffs, "lat", split_axis=3, concat_axis=0, tiled=True)
    first_slot = lax.axis_index("lat") * slots_here
    my_orders = lax.dynamic_slice_in_dim(order_table, first_slot, slots_here)
    tables = lax.map(legendre_rows, my_orders)
    weighted = (tables * fejer_weights()[None, None, :]).astype(jnp.bfloat16)
    plain_table = tables.astype(jnp.bfloat16)
    spectra = jnp.einsum(
        "rcpm,mkr->mpck", owned_coeffs, weighted, preferred_element_type=jnp.float32
    ).astype(jnp.bfloat16)
    gathered = lax.all_gather(spectra, "chan", axis=2, tiled=True)
    blocks = mixing_blocks(spectral_weight)
    mixed_spec = jnp.einsum(
        "mpck,mpqdc->mqdk", gathered, blocks, preferred_element_type=jnp.float32
    ).astype(jnp.bfloat16)
    synthesis = jnp.einsum(
        "mqdk,mkr->rdqm", mixed_spec, plain_table, preferred_element_type=jnp.float32
    ).astype(jnp.bfloat16)
    rows_back = lax.all_to_all(synthesis, "lat", split_axis=0, concat_axis=3, tiled=True)
    spatial = jnp.dot(
        rows_back.reshape(local_rows * local_channels, 2 * MODES),
        inverse,
        preferred_element_type=jnp.float32,
    )
    spatial = spatial.reshape(local_rows, local_channels, NLON)
    hidden = (ocean_state.astype(jnp.float32) + spatial).astype(jnp.bfloat16)
    points = lax.all_to_all(hidden, "chan", split_axis=2, concat_axis=1, tiled=True)
    inner_full, outer_full = (
        lax.all_gather(inner_weight, "chan", axis=1, tiled=True),
        lax.all_gather(outer_weight, "chan", axis=0, tiled=True),
    )
    pre_act = jnp.einsum("rcp,ch->rph", points, inner_full, preferred_element_type=jnp.float32)
    activated = jax.nn.gelu(pre_act).astype(jnp.bfloat16)
    update = jnp.einsum("rph,hc->rpc", activated, outer_full, preferred_element_type=jnp.float32)
    ocean_mask = land_mask.astype(jnp.float32)
    residual_part = jnp.transpose(points, (0, 2, 1)).astype(jnp.float32)
    return (ocean_mask[:, :, None] * (residual_part + update)).astype(jnp.bfloat16)


def solution(mesh):
    placed = (
        P("lat", "chan", None),
        P("lat", "chan"),
        P(),
        P("lat", None, "chan", None),
        P(None, "chan"),
        P("chan", None),
    )
    return jax.shard_map(
        local, mesh=mesh, in_specs=placed, out_specs=P("lat", "chan", None), check_vma=False
    )
```

profile of v0, /device:TPU:0, one launch (start us, length us, event | category | flops | bytes accessed | tf_op | source)
XLA Modules:
  0.0 1467.7 jit_solution(10121995507402593260)
XLA Ops:
  7.2 11.2 multiply_convert_fusion.2
  18.4 10.6 fusion.83
  29.0 3.6 copy.80
  32.6 11.8 copy.57
  44.3 7.4 all-to-all-start
  53.2 932.7 %while.13 = (s32[]{:T(128)}, f32[24,384,384]{2,1,0:T(8,128)}, s32[24]{0:T(128)}, s32[]{:T(128)}, f32[]{:T(128)}, /*index=5*/f32[]{:T(128)}, f32[]{:T(128)}) while((s32[]{:T(128)}, f32[24,384,384]{2,1,0:T(8,128)}, s32[24]{0:T(128)}, s32[]{:T(128)}, f32[]{:T(128)}, /*index=5*/f32[]{:T(128)}, f32[]{:T(128)}) %tuple.122), condition=%wide.region_20.21_spmd, body=%wide.region_0.20_spmd.sunk | while | flops 9975949 | bytes 54367292 | solution.py:113
  73.2 2.9 pad.1097
  112.0 2.9 pad.1097
  150.9 2.9 pad.1097
  189.7 2.9 pad.1097
  228.6 2.9 pad.1097
  267.4 2.9 pad.1097
  306.3 2.9 pad.1097
  345.1 2.9 pad.1097
  383.9 2.9 pad.1097
  422.8 2.9 pad.1097
  461.6 2.9 pad.1097
  500.5 2.9 pad.1097
  539.3 2.9 pad.1097
  578.2 2.9 pad.1097
  617.0 2.9 pad.1097
  655.9 2.9 pad.1097
  694.8 2.9 pad.1097
  733.6 2.9 pad.1097
  772.5 2.9 pad.1097
  811.3 2.9 pad.1097
  850.1 2.9 pad.1097
  889.0 2.9 pad.1097
  927.8 2.9 pad.1097
  966.7 2.9 pad.1097
  987.1 3.6 copy.58
  990.6 3.4 copy.59
  994.0 11.3 convert_bitcast_fusion.1
  1005.4 1.9 copy-done.10
  1007.4 2.0 maximum_bitcast_fusion.1
  1009.5 115.3 %all-gather.2.cloned.1.call-done = bf16[24,2,256,384]{2,3,1,0:T(8,128)(2,1)} async-done(((bf16[24,2,128,384]{2,3,1,0:T(8,128)(2,1)}), bf16[24,2,256,384]{2,3,1,0:T(8,128)(2,1)}) %all-gather.2.cloned.1.call-update) | async-done | bytes 9437200 | tf_op jit(solution)/shard_map/all_gather | solution.py:119
  1124.8 10.3 fusion.55
  1135.0 11.7 convert_bitcast_fusion
  1146.7 9.4 copy.63
  1156.1 108.9 %all_to_all.51 = bf16[384,128,2,24]{1,2,3,0:T(2,128)(2,1)S(1)} all-to-all(bf16[384,128,2,24]{1,2,3,0:T(2,128)(2,1)} %copy.63), channel_id=1, replica_groups=mesh['lat'=16,'chan'=2] {'lat'}, dimensions={0} | all-to-all | bytes 9437184 | tf_op jit(solution)/shard_map/all_to_all | solution.py:127
  1267.2 9.6 add_convert_fusion
  1276.9 16.9 %copy.67 = bf16[24,128,1440]{1,0,2:T(8,128)(2,1)} copy(bf16[24,128,1440]{1,2,0:T(8,128)(2,1)S(1)} %add_convert_fusion) | data formatting | bytes 17694720 | tf_op jit(solution)/shard_map/convert_element_type | solution.py:134
  1293.7 7.2 all-to-all-start.2
  1301.0 101.3 %all_gather.10 = bf16[256,512]{1,0:T(8,128)(2,1)S(1)} all-gather(bf16[256,256]{1,0:T(8,128)(2,1)S(1)} %copy-done.19), channel_id=1, replica_groups=mesh['lat'=16,'chan'=2] {'chan'}, dimensions={1}, use_global_device_ids=true | all-gather | bytes 393216 | tf_op jit(solution)/shard_map/all_gather | solution.py:137
  1402.3 6.2 all_gather.11
  1408.5 14.2 copy.102
  1422.7 20.0 %all_to_all.47 = bf16[24,256,720]{1,2,0:T(8,128)(2,1)} reshape(bf16[24,2,128,720]{2,1,3,0:T(2,128)(2,1)} %bitcast.169) | data formatting | bytes 17694720 | tf_op jit(solution)/shard_map/all_to_all | solution.py:135
  1442.7 18.0 %fusion.52 = bf16[24,720,256]{2,1,0:T(8,128)(2,1)} fusion(bf16[24,256,720]{1,2,0:T(8,128)(2,1)} %all_to_all.47, f32[24,720]{1,0:T(8,128)S(1)} %convert_element_type.124, bf16[512,256]{1,0:T(8,128)(2,1)S(1)} %all_gather.11, bf16[256,512]{1,0:T(8,128)(2,1)S(1)} %all_gather.10), kind=kOutput, calls=%fused_computation.239 | convolution fusion | flops 9157017600 | bytes 18288128 | tf_op jit(solution)/shard_map/rph,hc->rpc/dot_general | solution.py:142
  (5763 shorter events, 810.7 us)
Async XLA Ops:
  44.3 942.7 %all-to-all-start = ((bf16[24,128,2,384]{1,2,0,3:T(2,128)(2,1)}), bf16[24,128,2,384]{1,2,0,3:T(2,128)(2,1)}, u32[]{:S(2)}, u32[]{:S(2)}) async-start(bf16[24,128,2,384]{1,2,0,3:T(2,128)(2,1)} %copy.57), calls=%async_computation | async-start | bytes 9437184 | tf_op jit(solution)/shard_map/all_to_all | solution.py:110
  51.8 1073.0 %all-gather.2.cloned.1.call-start = ((), (), s32[]{:S(2)}) async-start(), calls=%async_computation.3 | async-start | bytes 14155776 | tf_op jit(solution)/shard_map/all_gather | solution.py:119
  73.1 3.4 copy-start.1
  76.2 10.2 copy-start.4
  111.9 3.4 copy-start.1
  115.0 10.2 copy-start.4
  150.7 3.4 copy-start.1
  153.8 10.2 copy-start.4
  189.6 3.4 copy-start.1
  192.7 10.2 copy-start.4
  228.5 3.4 copy-start.1
  231.5 10.2 copy-start.4
  267.3 3.4 copy-start.1
  270.4 10.2 copy-start.4
  306.2 3.4 copy-start.1
  309.2 10.2 copy-start.4
  345.0 3.4 copy-start.1
  348.1 10.2 copy-start.4
  386.9 10.2 copy-start.4
  422.7 3.4 copy-start.1
  425.7 10.2 copy-start.4
  461.5 3.4 copy-start.1
  464.6 10.2 copy-start.4
  500.4 3.4 copy-start.1
  503.4 10.2 copy-start.4
  539.2 3.4 copy-start.1
  542.3 10.2 copy-start.4
  581.1 10.2 copy-start.4
  616.9 3.4 copy-start.1
  620.0 10.2 copy-start.4
  655.8 3.4 copy-start.1
  658.9 10.2 copy-start.4
  697.8 10.2 copy-start.4
  733.5 3.4 copy-start.1
  736.6 10.2 copy-start.4
  775.4 10.2 copy-start.4
  811.2 3.4 copy-start.1
  814.3 10.2 copy-start.4
  853.1 10.2 copy-start.4
  891.9 10.2 copy-start.4
  927.7 3.4 copy-start.1
  930.8 10.2 copy-start.4
  966.6 3.4 copy-start.1
  969.7 10.2 copy-start.4
  1293.7 7.2 copy-start.21
  1293.7 7.3 copy-start.19
  1293.7 108.6 %copy-start.20 = (bf16[256,256]{1,0:T(8,128)(2,1)S(1)}, bf16[256,256]{1,0:T(8,128)(2,1)}, u32[]{:S(2)}) copy-start(bf16[256,256]{1,0:T(8,128)(2,1)} %param.13) | copy-start | bytes 393220
  1293.7 114.8 %all-to-all-start.2 = ((bf16[24,128,1440]{1,0,2:T(8,128)(2,1)}), bf16[24,128,1440]{1,0,2:T(8,128)(2,1)}, u32[]{:S(2)}, u32[]{:S(2)}) async-start(bf16[24,128,1440]{1,0,2:T(8,128)(2,1)} %copy.67), calls=%async_computation.2 | async-start | bytes 17694720 | tf_op jit(solution)/shard_map/all_to_all | solution.py:135
  (345 other events, 229.6 us)
Sparse Core Ops, SparseCore 0:
  1005.5 119.2 all-gather.1
where the time goes:
time: 1490 us; the launch traced here: 1470 us
  local copies, waits for them, and re-layouts  563 us (38%)
  other arithmetic  414 us (28%)
  blocking collectives  216 us (14%)
  waiting for transfers between devices  115 us (8%)
  matrix products  71.4 us (5%)
  loops' own time  59 us (4%)
    while x840, local copies, waits for them, and re-layouts  257 us
    add x336, other arithmetic, compose(): return (product / largest, first_log + second_log + jnp.log(largest))  183 us
    all_gather x1, waiting for transfers between devices, local(): gathered = lax.all_gather(spectra, 'chan', axis=2, tiled=True)  115 us
    slice x1272, local copies, waits for them, and re-layouts, legendre_rows(): lax.associative_scan(compose, (matrix, log_scale), axis=1)  115 us
    all_to_all x1, blocking collectives, local(): lax.all_to_all(synthesis, 'lat', split_axis=0, concat_axis=3, tiled=True)  109 us
    all_gather x1, blocking collectives, local(): lax.all_gather(inner_weight, 'chan', axis=1, tiled=True)  101 us
    another operation x1, loops' own time, local(): tables = lax.map(legendre_rows, my_orders)  59 us
    add x384, other arithmetic, compose(): second_mat[0] * first_mat[0] + second_mat[1] * first_mat[2]  44.1 us

commit v1 on v0

--- a/solution.py
+++ b/solution.py
@@ -7,6 +7,18 @@
 NLAT = 384
 NLON = 1440
 MODES = 384
+
+
+def product_in_turn(shard, axis, dim, term):
+    peers, here = (lax.axis_size(axis), lax.axis_index(axis))
+    downward = [(i, (i - 1) % peers) for i in range(peers)]
+    extent = shard.shape[dim]
+    held = shard
+    running = term(held, here * extent)
+    for hop in range(1, peers):
+        held = lax.ppermute(held, axis, downward)
+        running = running + term(held, (here + hop) % peers * extent)
+    return running
 
 
 def fejer_weights():
@@ -116,10 +128,17 @@
     spectra = jnp.einsum(
         "rcpm,mkr->mpck", owned_coeffs, weighted, preferred_element_type=jnp.float32
     ).astype(jnp.bfloat16)
-    gathered = lax.all_gather(spectra, "chan", axis=2, tiled=True)
     blocks = mixing_blocks(spectral_weight)
-    mixed_spec = jnp.einsum(
-        "mpck,mpqdc->mqdk", gathered, blocks, preferred_element_type=jnp.float32
+    mixed_spec = product_in_turn(
+        spectra,
+        "chan",
+        2,
+        lambda shard, start: jnp.einsum(
+            "mpck,mpqdc->mqdk",
+            shard,
+            lax.dynamic_slice_in_dim(blocks, start, shard.shape[2], axis=4),
+            preferred_element_type=jnp.float32,
+        ),
     ).astype(jnp.bfloat16)
     synthesis = jnp.einsum(
         "mqdk,mkr->rdqm", mixed_spec, plain_table, preferred_element_type=jnp.float32

time: 1490 us -> 1460 us (0.980)
  waiting for transfers between devices: 115 us -> 92.7 us
    all_gather x1 -> x0, waiting for transfers between devices: 115 us -> none  [local(): gathered = lax.all_gather(spectra, 'chan', axis=2, tiled=True)]
    ppermute x0 -> x1, waiting for transfers between devices: none -> 92.7 us  [product_in_turn(): held = lax.ppermute(held, axis, downward)]
where the time goes in v1:
time: 1460 us; the launch traced here: 1440 us
  local copies, waits for them, and re-layouts  555 us (38%)
  other arithmetic  417 us (29%)
  blocking collectives  217 us (15%)
  waiting for transfers between devices  92.7 us (6%)
  matrix products  76.6 us (5%)
  loops' own time  62.9 us (4%)
  starting transfers between devices  16.7 us (1%)
    while x840, local copies, waits for them, and re-layouts  260 us
    add x336, other arithmetic, compose(): return (product / largest, first_log + second_log + jnp.log(largest))  184 us
    slice x1272, local copies, waits for them, and re-layouts, legendre_rows(): lax.associative_scan(compose, (matrix, log_scale), axis=1)  115 us
    all_to_all x1, blocking collectives, local(): lax.all_to_all(synthesis, 'lat', split_axis=0, concat_axis=3, tiled=True)  109 us
    all_gather x1, blocking collectives, local(): lax.all_gather(inner_weight, 'chan', axis=1, tiled=True)  101 us
    ppermute x1, waiting for transfers between devices, product_in_turn(): held = lax.ppermute(held, axis, downward)  92.7 us
    another operation x1, loops' own time, local(): tables = lax.map(legendre_rows, my_orders)  62.9 us
    add x384, other arithmetic, compose(): second_mat[0] * first_mat[0] + second_mat[1] * first_mat[2]  44.1 us

profile of v1, /device:TPU:0, one launch (start us, length us, event | category | flops | bytes accessed | tf_op | source)
XLA Modules:
  0.0 1438.4 jit_solution(4020693393407691791)
XLA Ops:
  0.7 11.2 multiply_convert_fusion.2
  11.8 10.2 fusion.90
  23.4 3.0 copy.47
  26.4 8.0 all-to-all-start
  35.8 943.1 %while.13 = (s32[]{:T(128)}, f32[24,384,384]{2,1,0:T(8,128)}, s32[24]{0:T(128)}, s32[]{:T(128)}, f32[]{:T(128)}, /*index=5*/f32[]{:T(128)}, f32[]{:T(128)}) while((s32[]{:T(128)}, f32[24,384,384]{2,1,0:T(8,128)}, s32[24]{0:T(128)}, s32[]{:T(128)}, f32[]{:T(128)}, /*index=5*/f32[]{:T(128)}, f32[]{:T(128)}) %tuple.125), condition=%wide.region_20.21_spmd, body=%wide.region_0.20_spmd.sunk | while | flops 9975949 | bytes 54367292 | solution.py:125
  51.2 1.8 slice.2652
  55.7 2.9 pad.1103
  90.4 1.8 slice.2652
  95.0 2.9 pad.1103
  134.3 2.9 pad.1103
  173.6 2.9 pad.1103
  212.9 2.9 pad.1103
  252.2 2.9 pad.1103
  291.4 2.9 pad.1103
  330.7 2.9 pad.1103
  370.0 2.9 pad.1103
  409.3 2.9 pad.1103
  448.6 2.9 pad.1103
  487.8 2.9 pad.1103
  527.1 2.9 pad.1103
  566.4 2.9 pad.1103
  605.7 2.9 pad.1103
  645.0 2.9 pad.1103
  684.4 2.9 pad.1103
  723.7 2.9 pad.1103
  762.9 2.9 pad.1103
  802.2 2.9 pad.1103
  841.5 2.9 pad.1103
  880.8 2.9 pad.1103
  920.1 2.9 pad.1103
  959.4 2.9 pad.1103
  980.0 5.9 copy.48
  985.8 11.2 fusion.87
  998.6 2.1 copy.106
  1003.5 5.4 fusion.75
  1008.9 92.7 %collective-permute-done = bf16[24,2,128,384]{2,3,1,0:T(8,128)(2,1)} collective-permute-done((bf16[24,2,128,384]{2,3,1,0:T(8,128)(2,1)}, bf16[24,2,128,384]{2,3,1,0:T(8,128)(2,1)}, u32[]{:S(2)}, u32[]{:S(2)}) %collective-permute-start) | collective-permute-done | bytes 4718624 | tf_op jit(solution)/shard_map/ppermute | solution.py:19
  1101.6 7.8 fusion.73
  1109.4 14.4 %convert_bitcast_fusion = bf16[384,128,2,24]{1,0,2,3:T(8,128)(2,1)} fusion(f32[24,384,384]{2,1,0:T(8,128)} %get-tuple-element.65, f32[24,2,128,384,1]{3,2,1,0,4:T(8,128)} %fusion.73, f32[24,2,128,384,1]{3,2,1,0,4:T(8,128)} %fusion.75), kind=kOutput, calls=%fused_computation.266 | convolution fusion | flops 1822556160 | bytes 37748736 | tf_op jit(solution)/shard_map/mqdk,mkr->rdqm/dot_general | solution.py:143
  1123.8 9.3 copy.53
  1133.1 109.0 %all_to_all.51 = bf16[384,128,2,24]{1,2,3,0:T(2,128)(2,1)S(1)} all-to-all(bf16[384,128,2,24]{1,2,3,0:T(2,128)(2,1)} %copy.53), channel_id=1, replica_groups=mesh['lat'=16,'chan'=2] {'lat'}, dimensions={0} | all-to-all | bytes 9437184 | tf_op jit(solution)/shard_map/all_to_all | solution.py:146
  1244.4 9.6 add_convert_fusion
  1254.0 16.9 %copy.57 = bf16[24,128,1440]{1,0,2:T(8,128)(2,1)} copy(bf16[24,128,1440]{1,2,0:T(8,128)(2,1)S(1)} %add_convert_fusion) | data formatting | bytes 17694720 | tf_op jit(solution)/shard_map/convert_element_type | solution.py:153
  1270.9 7.2 all-to-all-start.2
  1278.2 101.3 %all_gather.6 = bf16[256,512]{1,0:T(8,128)(2,1)S(1)} all-gather(bf16[256,256]{1,0:T(8,128)(2,1)S(1)} %copy-done.18), channel_id=1, replica_groups=mesh['lat'=16,'chan'=2] {'chan'}, dimensions={1}, use_global_device_ids=true | all-gather | bytes 393216 | tf_op jit(solution)/shard_map/all_gather | solution.py:156
  1379.5 6.2 all_gather.7
  1385.6 14.3 copy.105
  1400.0 20.0 %all_to_all.47 = bf16[24,256,720]{1,2,0:T(8,128)(2,1)} reshape(bf16[24,2,128,720]{2,1,3,0:T(2,128)(2,1)} %bitcast.183) | data formatting | bytes 17694720 | tf_op jit(solution)/shard_map/all_to_all | solution.py:154
  1419.9 18.0 %fusion.52 = bf16[24,720,256]{2,1,0:T(8,128)(2,1)} fusion(bf16[24,256,720]{1,2,0:T(8,128)(2,1)} %all_to_all.47, f32[24,720]{1,0:T(8,128)S(1)} %convert_element_type.124, bf16[512,256]{1,0:T(8,128)(2,1)S(1)} %all_gather.7, bf16[256,512]{1,0:T(8,128)(2,1)S(1)} %all_gather.6), kind=kOutput, calls=%fused_computation.239 | convolution fusion | flops 9157017600 | bytes 18288128 | tf_op jit(solution)/shard_map/rph,hc->rpc/dot_general | solution.py:161
  (5767 shorter events, 817.2 us)
Async XLA Ops:
  26.4 953.5 %all-to-all-start = ((bf16[24,128,2,384]{1,0,2,3:T(8,128)(2,1)}), bf16[24,128,2,384]{1,0,2,3:T(8,128)(2,1)}, u32[]{:S(2)}, u32[]{:S(2)}) async-start(bf16[24,128,2,384]{1,0,2,3:T(8,128)(2,1)} %copy.47), calls=%async_computation | async-start | bytes 9437184 | tf_op jit(solution)/shard_map/all_to_all | solution.py:122
  55.6 3.5 copy-start.1
  58.8 10.2 copy-start.4
  94.9 3.5 copy-start.1
  98.0 10.2 copy-start.4
  134.2 3.5 copy-start.1
  137.3 10.2 copy-start.4
  173.5 3.5 copy-start.1
  176.6 10.2 copy-start.4
  212.8 3.5 copy-start.1
  215.9 10.2 copy-start.4
  252.1 3.5 copy-start.1
  255.2 10.2 copy-start.4
  291.3 3.5 copy-start.1
  294.5 10.2 copy-start.4
  330.6 3.5 copy-start.1
  333.7 10.2 copy-start.4
  369.9 3.5 copy-start.1
  373.0 10.2 copy-start.4
  412.3 10.2 copy-start.4
  448.5 3.5 copy-start.1
  451.6 10.2 copy-start.4
  487.7 3.5 copy-start.1
  490.9 10.2 copy-start.4
  527.0 3.5 copy-start.1
  530.2 10.2 copy-start.4
  569.4 10.2 copy-start.4
  605.6 3.5 copy-start.1
  608.7 10.2 copy-start.4
  644.9 3.5 copy-start.1
  648.1 10.2 copy-start.4
  687.4 10.2 copy-start.4
  723.5 3.5 copy-start.1
  726.7 10.2 copy-start.4
  766.0 10.2 copy-start.4
  802.1 3.5 copy-start.1
  805.2 10.2 copy-start.4
  844.5 10.2 copy-start.4
  883.8 10.2 copy-start.4
  919.9 3.5 copy-start.1
  923.1 10.2 copy-start.4
  959.3 3.5 copy-start.1
  962.4 10.2 copy-start.4
  997.1 104.5 %collective-permute-start = (bf16[24,2,128,384]{2,3,1,0:T(8,128)(2,1)}, bf16[24,2,128,384]{2,3,1,0:T(8,128)(2,1)}, u32[]{:S(2)}, u32[]{:S(2)}) collective-permute-start(bf16[24,2,128,384]{2,3,1,0:T(8,128)(2,1)} %bitcast.180), channel_id=1, source_target_pairs={{0,1},{1,0},{2,3},{3,2},{4,5},{5,4},{6,7},{7,6},{8,9},{9,8},{10,11... | collective-permute-start | bytes 14155784 | tf_op jit(solution)/shard_map/ppermute | solution.py:19
  1270.9 7.2 copy-start.20
  1270.9 7.3 copy-start.18
  1270.9 108.6 %copy-start.19 = (bf16[256,256]{1,0:T(8,128)(2,1)S(1)}, bf16[256,256]{1,0:T(8,128)(2,1)}, u32[]{:S(2)}) copy-start(bf16[256,256]{1,0:T(8,128)(2,1)} %param.13) | copy-start | bytes 393220
  1270.9 114.8 %all-to-all-start.2 = ((bf16[24,128,1440]{1,0,2:T(8,128)(2,1)}), bf16[24,128,1440]{1,0,2:T(8,128)(2,1)}, u32[]{:S(2)}, u32[]{:S(2)}) async-start(bf16[24,128,1440]{1,0,2:T(8,128)(2,1)} %copy.57), calls=%async_computation.2 | async-start | bytes 17694720 | tf_op jit(solution)/shard_map/all_to_all | solution.py:154
  (346 other events, 232.9 us)
